TPU v7x, 128 devices: a whole 4x4x4 slice. The times are simulated.
128 devices in a mesh: vert: 64 (over z, y_hi, x, core), row: 2 (over y_lo).
Axes of the slice: x: 4, y: 4 (y_hi: 2, y_lo: 2; y = y_hi * 2 + y_lo), z: 4, core: 2. Of those that a mesh axis runs over, the one named last changes fastest.
Arguments:
- features: float32 [524288, 256], P(('vert', 'row')), may hold values from -6 to 6
- w_self: float32 [256, 256], replicated, may hold values from -0.375 to 0.375
- w_neigh: float32 [256, 256], replicated, may hold values from -0.75 to 0.75
- bias: float32 [256], replicated, may hold values from -3 to 3
- w_head: float32 [256], replicated, may hold values from -0.75 to 0.75
- tile_weights: float32 [16384, 128, 128], P(('vert', 'row')), may hold values from 0.01 to 1
- tile_dst: int32 [16384], P(('vert', 'row')), may hold values from 0 to 31
- tile_src: int32 [16384], P(('vert', 'row')), may hold values from 0 to 167
- tile_count: int32 [128], P(('vert', 'row')), may hold values from 16 to 128, as said below
- hub_block: int32 [128], P(('vert', 'row')), may hold values from 0 to 31
- send_rows: int32 [128, 128, 8], P(('vert', 'row')), may hold values from 0 to 4095
- send_count: int32 [128, 128], P(('vert', 'row')), may hold values from 1 to 8, as said below
- labels: int32 [524288], P(('vert', 'row')), may hold values from 0 to 1
Outputs:
- grad_self: float32 [256, 256], replicated
- grad_neigh: float32 [256, 256], replicated
- grad_bias: float32 [256], replicated
- grad_head: float32 [256], replicated
Inputs may be any that keep to these rules, and one draw needn't show every extreme that they name: Tile t of a device is used when t < its tile_count; some device uses all 128 tiles and some 128 // 8. `send_count`: each sending device fills all 8 slots for at least one receiving device.
All inputs are finite; a program needn't handle non-finite values.
Results may differ from a plain program's by a relative error of at most 0.0003.
Values sent between devices are 32-bit elements; how exact they have to be, the bound alone decides.
A program may use at most 128 MiB of HBM per device.

v0:
```python
import math
import jax
import jax.numpy as jnp
from jax import lax
from jax.sharding import PartitionSpec as P

FULL_PRECISION = lax.Precision.HIGHEST


def on_device(
    features,
    w_self,
    w_neigh,
    bias,
    w_head,
    tile_weights,
    tile_dst,
    tile_src,
    tile_count,
    hub_block,
    send_rows,
    send_count,
    labels,
):
    tile_size = tile_weights.shape[1]
    tile_total = tile_weights.shape[0]
    feature_width = features.shape[1]
    block_count = features.shape[0] // tile_size
    slot_count = send_rows.shape[2]
    own_blocks = features.reshape(block_count, tile_size, feature_width)
    hub_local = lax.dynamic_slice_in_dim(own_blocks, hub_block[0], 1, 0)
    hub_blocks = lax.all_gather(hub_local, ("vert", "row"), axis=0, tiled=True)
    outgoing = features[send_rows[0]]
    slot_index = jnp.arange(slot_count, dtype=jnp.int32)
    alive = slot_index[None, :] < send_count[0][:, None]
    outgoing = jnp.where(alive[:, :, None], outgoing, jnp.zeros_like(outgoing))
    incoming = lax.all_to_all(outgoing, ("vert", "row"), split_axis=0, concat_axis=0, tiled=True)
    source_table = jnp.concatenate(
        [own_blocks, incoming.reshape(-1, tile_size, feature_width), hub_blocks], 0
    )
    active = jnp.arange(tile_total, dtype=jnp.int32) < tile_count[0]
    picked = source_table[tile_src]
    contrib = jnp.einsum("tij,tjf->tif", tile_weights, picked, precision=FULL_PRECISION)
    block_ids = jnp.arange(block_count, dtype=jnp.int32)
    selector = ((tile_dst[None, :] == block_ids[:, None]) & active[None, :]).astype(features.dtype)
    summed = jnp.einsum("bt,tif->bif", selector, contrib, precision=FULL_PRECISION)
    weight_sum = jnp.einsum(
        "bt,ti->bi", selector, jnp.sum(tile_weights, axis=2), precision=FULL_PRECISION
    )
    neigh_mean = ((own_blocks + summed) / (1.0 + weight_sum)[:, :, None]).reshape(-1, feature_width)
    pre_act = (
        jnp.dot(features, w_self, precision=FULL_PRECISION)
        + jnp.dot(neigh_mean, w_neigh, precision=FULL_PRECISION)
        + bias[None, :]
    )
    sigmoid_pre = jax.nn.sigmoid(pre_act)
    hidden = pre_act * sigmoid_pre
    head_score = jnp.dot(hidden, w_head, precision=FULL_PRECISION)
    target = 2.0 * labels.astype(features.dtype) - 1.0
    vertex_total = features.shape[0] * lax.axis_size(("vert", "row"))
    loss_scale = 1.0 / math.sqrt(vertex_total)
    dscore = (head_score - target) * loss_scale
    dpre = dscore[:, None] * w_head[None, :] * (sigmoid_pre * (1.0 + pre_act * (1.0 - sigmoid_pre)))
    local_self = jnp.dot(features.T, dpre, precision=FULL_PRECISION)
    local_neigh = jnp.dot(neigh_mean.T, dpre, precision=FULL_PRECISION)
    local_bias = jnp.sum(dpre, axis=0)
    local_head = jnp.dot(hidden.T, dscore, precision=FULL_PRECISION)
    grad_self, grad_neigh, grad_bias, grad_head = lax.psum(
        (local_self, local_neigh, local_bias, local_head), ("vert", "row")
    )
    return (grad_self, grad_neigh, grad_bias, grad_head)


def solution(mesh):
    in_specs = (
        P(("vert", "row"), None),
        P(),
        P(),
        P(),
        P(),
        P(("vert", "row"), None, None),
        P(("vert", "row")),
        P(("vert", "row")),
        P(("vert", "row")),
        P(("vert", "row")),
        P(("vert", "row"), None, None),
        P(("vert", "row"), None),
        P(("vert", "row")),
    )
    out_specs = (P(), P(), P(), P())
    return jax.shard_map(
        on_device, mesh=mesh, in_specs=in_specs, out_specs=out_specs, check_vma=False
    )
```

profile of v0, /device:TPU:1, one launch (start us, length us, event | category | flops | bytes accessed | tf_op | source)
XLA Modules:
  0.0 630.4 jit_solution(8257241849353653896)
XLA Ops:
  7.9 1.6 constant_dynamic-slice_fusion
  10.4 5.7 gather_fusion
  16.2 1.2 bitcast_select_fusion
  17.4 11.5 %all-to-all-start = ((f32[128,8,256]{2,1,0:T(8,128)}), f32[128,8,256]{2,1,0:T(8,128)S(1)}, u32[]{:S(2)}, u32[]{:S(2)}) async-start(f32[128,8,256]{2,1,0:T(8,128)} %bitcast_select_fusion), calls=%async_computation | async-start | bytes 2097152 | tf_op jit(solution)/shard_map/all_to_all | solution.py:37
  29.6 5.6 reduce_sum.18
  35.6 7.6 %fusion.21 = f32[4096,256]{1,0:T(8,128)} fusion(f32[4096,256]{1,0:T(8,128)} %param.13, f32[256,256]{1,0:T(8,128)S(1)} %copy-done), kind=kOutput, calls=%fused_computation.41 | convolution fusion | flops 3221225472 | bytes 8650752 | tf_op jit(solution)/shard_map/dot_general | solution.py:52
  43.2 8.0 %all-to-all-done = f32[128,8,256]{2,1,0:T(8,128)S(1)} async-done(((f32[128,8,256]{2,1,0:T(8,128)}), f32[128,8,256]{2,1,0:T(8,128)S(1)}, u32[]{:S(2)}, u32[]{:S(2)}) %all-to-all-start) | async-done | bytes 1048608 | tf_op jit(solution)/shard_map/all_to_all | solution.py:37
  51.2 294.8 %all-gather.2.cloned.1.call-done = f32[128,128,256]{2,1,0:T(8,128)} async-done(((f32[1,128,256]{2,1,0:T(8,128)}), f32[128,128,256]{2,1,0:T(8,128)}) %all-gather.2.cloned.1.call-update) | async-done | bytes 16777232 | tf_op jit(solution)/shard_map/all_gather | solution.py:32
  346.0 15.9 %pad_maximum_fusion = f32[168,128,256]{2,1,0:T(8,128)} fusion(f32[128,128,256]{2,1,0:T(8,128)} %all-gather.2.cloned.1.call-done, f32[8,128,256]{2,1,0:T(8,128)S(1)} %bitcast.58, f32[32,128,256]{2,1,0:T(8,128)} %bitcast.54), kind=kLoop, calls=%fused_computation.2 | loop fusion | flops 11010048 | bytes 44040192 | tf_op jit(solution)/shard_map/concatenate | solution.py:38
  362.0 17.3 %gather_fusion.1 = f32[128,128,256]{2,1,0:T(8,128)} fusion(f32[168,128,256]{2,1,0:T(8,128)} %pad_maximum_fusion, s32[1024]{0:T(1024)S(1)} %pad_clamp_fusion), kind=kCustom, calls=%fused_computation.1 | custom fusion | bytes 33554944 | tf_op jit(solution)/shard_map/gather | solution.py:42
  379.3 34.3 %convolution_bitcast_fusion = f32[128,128,256]{1,2,0:T(8,128)} fusion(f32[128,128,256]{2,1,0:T(8,128)} %gather_fusion.1, f32[128,128,128]{2,1,0:T(8,128)} %param.18), kind=kOutput, calls=%fused_computation.3 | convolution fusion | flops 6442450944 | bytes 41943040 | tf_op jit(solution)/shard_map/tij,tjf->tif/dot_general | solution.py:43
  413.6 17.7 %copy.26 = f32[128,128,256]{2,0,1:T(8,128)} copy(f32[128,128,256]{1,2,0:T(8,128)} %convolution_bitcast_fusion) | data formatting | bytes 33554432 | tf_op jit(solution)/shard_map/tij,tjf->tif/dot_general | solution.py:43
  431.2 13.7 %fusion.4 = f32[32,128,256]{2,0,1:T(8,128)S(1)} fusion(f32[32,128,256]{2,1,0:T(8,128)} %bitcast.55, f32[128,128,256]{2,0,1:T(8,128)} %copy.26, f32[32,128]{0,1:T(8,128)S(1)} %copy.28, s32[128]{0:T(128)S(1)} %copy-done.7, pred[128]{0:T(512)(128)(4,1)S(1)} %iota_compare_fusion.2), kind=kOutput, calls=%fused_computation.12 | convolution fusion | flops 1612718080 | bytes 25182848 | tf_op jit(solution)/shard_map/bt,tif->bif/dot_general | solution.py:46
  445.0 2.4 copy.29
  447.5 3.4 fusion
  450.9 4.4 fusion.5
  455.4 2.4 fusion.20
  457.9 7.5 %fusion.22 = f32[256,256]{1,0:T(8,128)} fusion(f32[4096,256]{1,0:T(8,128)S(1)} %bitcast.57, f32[4096,256]{1,0:T(8,128)S(1)} %get-tuple-element.21), kind=kOutput, calls=%fused_computation.42 | convolution fusion | flops 3221225472 | bytes 8650752 | tf_op jit(solution)/shard_map/dot_general | solution.py:65
  465.4 7.7 %convolution_bitcast_fusion.1 = f32[256,256]{0,1:T(8,128)} fusion(f32[4096,256]{1,0:T(8,128)S(1)} %get-tuple-element.21, f32[4096,256]{1,0:T(8,128)S(1)} %copy-done.2), kind=kOutput, calls=%fused_computation.20 | convolution fusion | flops 3221225472 | bytes 8650752 | tf_op jit(solution)/shard_map/dot_general | solution.py:64
  473.1 5.2 fusion.7
  478.2 67.7 %all-reduce = (f32[256]{0:T(256)}, f32[256]{0:T(256)}) all-reduce(f32[256]{0:T(256)S(1)} %get-tuple-element.20, f32[256]{0:T(256)S(1)} %bitcast.62), channel_id=1, replica_groups=mesh['vert'=64,'row'=2] {'vert','row'}, use_global_device_ids=true, to_apply=%region_4.5 | all-reduce | flops 512 | bytes 4096 | tf_op jit(solution)/shard_map/psum | solution.py:68
  545.9 74.0 %all-reduce.4.cloned.1.call-done = (f32[256,256]{0,1:T(8,128)}, f32[256,256]{1,0:T(8,128)}) async-done(((f32[256,256]{0,1:T(8,128)}, f32[256,256]{1,0:T(8,128)}), (f32[256,256]{0,1:T(8,128)}, f32[256,256]{1,0:T(8,128)})) %all-reduce.4.cloned.1.call-update) | async-done | bytes 524304 | tf_op jit(solution)/shard_map/psum | solution.py:68
  619.9 1.8 copy.30
  621.7 1.7 copy.39
  (39 shorter events, 1.5 us)
Async XLA Ops:
  7.2 28.4 %copy-start = (f32[256,256]{1,0:T(8,128)S(1)}, f32[256,256]{1,0:T(8,128)}, u32[]{:S(2)}) copy-start(f32[256,256]{1,0:T(8,128)} %param.14) | copy-start | bytes 786436
  7.2 338.9 %all-gather.2.cloned.1.call-start = ((), (), s32[]{:S(2)}) async-start(), calls=%async_computation.1 | async-start | bytes 16908288 | tf_op jit(solution)/shard_map/all_gather | solution.py:32
  10.4 5.7 copy-start.10
  17.4 33.8 %all-to-all-start = ((f32[128,8,256]{2,1,0:T(8,128)}), f32[128,8,256]{2,1,0:T(8,128)S(1)}, u32[]{:S(2)}, u32[]{:S(2)}) async-start(f32[128,8,256]{2,1,0:T(8,128)} %bitcast_select_fusion), calls=%async_computation | async-start | bytes 2097152 | tf_op jit(solution)/shard_map/all_to_all | solution.py:37
  28.9 591.0 %all-reduce.4.cloned.1.call-start = ((), (), s32[]{:S(2)}) async-start(), calls=%async_computation.2 | async-start | bytes 1048576 | tf_op jit(solution)/shard_map/psum | solution.py:68
  29.6 5.7 copy-start.7
  29.6 5.9 copy-start.11
  445.0 2.5 copy-start.4
  445.0 2.5 copy-start.5
  445.0 2.5 copy-start.8
  447.5 3.5 copy-start.9
  450.9 4.5 copy-start.3
  450.9 4.5 copy-start.6
  457.9 7.5 %copy-start.2 = (f32[4096,256]{1,0:T(8,128)S(1)}, f32[4096,256]{1,0:T(8,128)}, u32[]{:S(2)}) copy-start(f32[4096,256]{1,0:T(8,128)} %param.13) | copy-start | bytes 12582916
  473.1 150.3 %copy-start.1 = (f32[256,256]{1,0:T(8,128)S(1)}, f32[256,256]{1,0:T(8,128)}, u32[]{:S(2)}) copy-start(f32[256,256]{1,0:T(8,128)} %param.14) | copy-start | bytes 786436
Sparse Core Ops, SparseCore 0:
  10.3 335.7 all-gather.1
  473.2 146.6 all-reduce.3
where the time goes:
time: 636 us; the launch traced here: 630 us
  waiting for transfers between devices  377 us (59%)
  matrix products  83.9 us (13%)
  blocking collectives  67.7 us (11%)
  local copies, waits for them, and re-layouts  48.4 us (8%)
  other arithmetic  26 us (4%)
  between operations  15.9 us (2%)
  starting transfers between devices  11.6 us (2%)
    all_gather x1, waiting for transfers between devices, on_device(): hub_blocks = lax.all_gather(hub_local, ('vert', 'row'), axis=0, tiled=True)  295 us
    psum x1, waiting for transfers between devices, on_device(): lax.psum((local_self, local_neigh, local_bias, local_head), ('vert', 'row'))  74 us
    psum x1, blocking collectives, on_device(): lax.psum((local_self, local_neigh, local_bias, local_head), ('vert', 'row'))  67.7 us
    dot_general x1, matrix products, on_device(): jnp.einsum('tij,tjf->tif', tile_weights, picked, precision=FULL_PRECISION)  34.3 us
    dot_general x1, local copies, waits for them, and re-layouts, on_device(): jnp.einsum('tij,tjf->tif', tile_weights, picked, precision=FULL_PRECISION)  17.7 us
    gather x1, local copies, waits for them, and re-layouts, on_device(): picked = source_table[tile_src]  17.3 us
    concatenate x1, other arithmetic, on_device(): jnp.concatenate([own_blocks, incoming.reshape(-1, tile_size, feature_widt...  15.9 us
    dot_general x1, matrix products, on_device(): jnp.einsum('bt,tif->bif', selector, contrib, precision=FULL_PRECISION)  13.7 us
  transfers between devices with their start and end apart: 3, of which 3 were waited for; matrix products, arithmetic and copies ran while one was open for 4% of the time, Pallas kernels for 0%

commit v1 on v0

--- a/solution.py
+++ b/solution.py
@@ -66,7 +66,7 @@
     local_bias = jnp.sum(dpre, axis=0)
     local_head = jnp.dot(hidden.T, dscore, precision=FULL_PRECISION)
     grad_self, grad_neigh, grad_bias, grad_head = lax.psum(
-        (local_self, local_neigh, local_bias, local_head), ("vert", "row")
+        lax.psum((local_self, local_neigh, local_bias, local_head), "row"), "vert"
     )
     return (grad_self, grad_neigh, grad_bias, grad_head)
 

time: 636 us -> 1160 us (1.82)
  waiting for transfers between devices: 377 us -> 802 us
  blocking collectives: 67.7 us -> 168 us
    psum x1 -> x2, waiting for transfers between devices: 74 us -> 499 us  [the longest x1 463 us: on_device(): lax.psum(lax.psum((local_self, local_neigh, local_bias, local_head), 'row...]
    psum x1 -> x2, blocking collectives: 67.7 us -> 168 us  [the longest x1 164 us: on_device(): lax.psum(lax.psum((local_self, local_neigh, local_bias, local_head), 'row...]
  transfers between devices with their start and end apart: 3 -> 4, of which waited for: 3 -> 4; matrix products, arithmetic and copies ran while one was open for 4% -> 2% of each run, Pallas kernels for 0% -> 0%
where the time goes in v1:
time: 1160 us
  waiting for transfers between devices  802 us (69%)
  blocking collectives  168 us (14%)
  matrix products  83.9 us (7%)
  local copies, waits for them, and re-layouts  48.4 us (4%)
  other arithmetic  26 us (2%)
  between operations  15.6 us (1%)
  starting transfers between devices  11.6 us (1%)
    psum x1, waiting for transfers between devices, on_device(): lax.psum(lax.psum((local_self, local_neigh, local_bias, local_head), 'row...  463 us
    all_gather x1, waiting for transfers between devices, on_device(): hub_blocks = lax.all_gather(hub_local, ('vert', 'row'), axis=0, tiled=True)  295 us
    psum x1, blocking collectives, on_device(): lax.psum(lax.psum((local_self, local_neigh, local_bias, local_head), 'row...  164 us
    psum x1, waiting for transfers between devices, on_device(): lax.psum((local_self, local_neigh, local_bias, local_head), 'row')  36.6 us
    dot_general x1, matrix products, on_device(): jnp.einsum('tij,tjf->tif', tile_weights, picked, precision=FULL_PRECISION)  34.3 us
  transfers between devices with their start and end apart: 4, of which 4 were waited for; matrix products, arithmetic and copies ran while one was open for 2% of the time, Pallas kernels for 0%

profile of v1, /device:TPU:1, one launch (start us, length us, event | category | flops | bytes accessed | tf_op | source)
XLA Modules:
  0.0 1155.7 jit_solution(16953007655406878660)
XLA Ops:
  10.4 5.7 gather_fusion
  17.4 11.5 all-to-all-start
  29.6 5.6 reduce_sum.18
  35.6 7.6 fusion.21
  43.2 8.0 all-to-all-done
  51.2 294.8 %all-gather.2.cloned.1.call-done = f32[128,128,256]{2,1,0:T(8,128)} async-done(((f32[1,128,256]{2,1,0:T(8,128)}), f32[128,128,256]{2,1,0:T(8,128)}) %all-gather.2.cloned.1.call-update) | async-done | bytes 16777232 | tf_op jit(solution)/shard_map/all_gather | solution.py:32
  346.0 15.9 %pad_maximum_fusion = f32[168,128,256]{2,1,0:T(8,128)} fusion(f32[128,128,256]{2,1,0:T(8,128)} %all-gather.2.cloned.1.call-done, f32[8,128,256]{2,1,0:T(8,128)S(1)} %bitcast.58, f32[32,128,256]{2,1,0:T(8,128)} %bitcast.54), kind=kLoop, calls=%fused_computation.2 | loop fusion | flops 11010048 | bytes 44040192 | tf_op jit(solution)/shard_map/concatenate | solution.py:38
  362.0 17.3 %gather_fusion.1 = f32[128,128,256]{2,1,0:T(8,128)} fusion(f32[168,128,256]{2,1,0:T(8,128)} %pad_maximum_fusion, s32[1024]{0:T(1024)S(1)} %pad_clamp_fusion), kind=kCustom, calls=%fused_computation.1 | custom fusion | bytes 33554944 | tf_op jit(solution)/shard_map/gather | solution.py:42
  379.3 34.3 %convolution_bitcast_fusion = f32[128,128,256]{1,2,0:T(8,128)} fusion(f32[128,128,256]{2,1,0:T(8,128)} %gather_fusion.1, f32[128,128,128]{2,1,0:T(8,128)} %param.18), kind=kOutput, calls=%fused_computation.3 | convolution fusion | flops 6442450944 | bytes 41943040 | tf_op jit(solution)/shard_map/tij,tjf->tif/dot_general | solution.py:43
  413.6 17.7 %copy.26 = f32[128,128,256]{2,0,1:T(8,128)} copy(f32[128,128,256]{1,2,0:T(8,128)} %convolution_bitcast_fusion) | data formatting | bytes 33554432 | tf_op jit(solution)/shard_map/tij,tjf->tif/dot_general | solution.py:43
  431.2 13.7 %fusion.4 = f32[32,128,256]{2,0,1:T(8,128)S(1)} fusion(f32[32,128,256]{2,1,0:T(8,128)} %bitcast.55, f32[128,128,256]{2,0,1:T(8,128)} %copy.26, f32[32,128]{0,1:T(8,128)S(1)} %copy.28, s32[128]{0:T(128)S(1)} %copy-done.7, pred[128]{0:T(512)(128)(4,1)S(1)} %iota_compare_fusion.2), kind=kOutput, calls=%fused_computation.12 | convolution fusion | flops 1612718080 | bytes 25182848 | tf_op jit(solution)/shard_map/bt,tif->bif/dot_general | solution.py:46
  445.0 2.4 copy.29
  447.5 3.4 fusion
  450.9 4.4 fusion.5
  455.4 2.4 fusion.20
  457.9 7.5 fusion.22
  465.4 7.7 convolution_bitcast_fusion.1
  473.1 36.6 %all-reduce.9.cloned.1.call-done = (f32[256,256]{0,1:T(8,128)}, f32[256,256]{1,0:T(8,128)}) async-done(((f32[256,256]{0,1:T(8,128)}, f32[256,256]{1,0:T(8,128)}), (f32[256,256]{0,1:T(8,128)}, f32[256,256]{1,0:T(8,128)})) %all-reduce.9.cloned.1.call-update) | async-done | bytes 524304 | tf_op jit(solution)/shard_map/psum | solution.py:69
  509.8 5.2 fusion.7
  514.9 3.8 all-reduce.2
  518.7 164.3 %all-reduce = (f32[256]{0:T(256)}, f32[256]{0:T(256)}) all-reduce(f32[256]{0:T(256)S(1)} %get-tuple-element.20, f32[256]{0:T(256)S(1)} %get-tuple-element.21), channel_id=1, replica_groups=mesh['vert'=64,'row'=2] {'vert'}, use_global_device_ids=true, to_apply=%region_7.8 | all-reduce | flops 512 | bytes 4096 | tf_op jit(solution)/shard_map/psum | solution.py:68
  683.0 462.5 %all-reduce.7.cloned.1.call-done = (f32[256,256]{0,1:T(8,128)}, f32[256,256]{1,0:T(8,128)}) async-done(((f32[256,256]{0,1:T(8,128)}, f32[256,256]{1,0:T(8,128)}), (f32[256,256]{0,1:T(8,128)}, f32[256,256]{1,0:T(8,128)})) %all-reduce.7.cloned.1.call-update) | async-done | bytes 524304 | tf_op jit(solution)/shard_map/psum | solution.py:68
  1145.5 1.8 copy.30
  1147.2 1.7 copy.41
  (43 shorter events, 4.3 us)
Async XLA Ops:
  7.2 28.4 %copy-start = (f32[256,256]{1,0:T(8,128)S(1)}, f32[256,256]{1,0:T(8,128)}, u32[]{:S(2)}) copy-start(f32[256,256]{1,0:T(8,128)} %param.14) | copy-start | bytes 786436
  7.2 338.9 %all-gather.2.cloned.1.call-start = ((), (), s32[]{:S(2)}) async-start(), calls=%async_computation.1 | async-start | bytes 16908288 | tf_op jit(solution)/shard_map/all_gather | solution.py:32
  10.4 5.7 copy-start.10
  17.4 33.8 %all-to-all-start = ((f32[128,8,256]{2,1,0:T(8,128)}), f32[128,8,256]{2,1,0:T(8,128)S(1)}, u32[]{:S(2)}, u32[]{:S(2)}) async-start(f32[128,8,256]{2,1,0:T(8,128)} %bitcast_select_fusion), calls=%async_computation | async-start | bytes 2097152 | tf_op jit(solution)/shard_map/all_to_all | solution.py:37
  28.9 480.9 %all-reduce.9.cloned.1.call-start = ((), (), s32[]{:S(2)}) async-start(), calls=%async_computation.3 | async-start | bytes 1048576 | tf_op jit(solution)/shard_map/psum | solution.py:69
  29.6 5.7 copy-start.7
  29.6 5.9 copy-start.11
  445.0 2.5 copy-start.4
  445.0 2.5 copy-start.5
  445.0 2.5 copy-start.8
  447.5 3.5 copy-start.9
  450.9 4.5 copy-start.3
  450.9 4.5 copy-start.6
  457.9 7.5 copy-start.2
  473.1 672.4 %all-reduce.7.cloned.1.call-start = ((), (), s32[]{:S(2)}) async-start(), calls=%async_computation.2 | async-start | bytes 1048576 | tf_op jit(solution)/shard_map/psum | solution.py:68
  509.8 639.2 %copy-start.1 = (f32[256,256]{1,0:T(8,128)S(1)}, f32[256,256]{1,0:T(8,128)}, u32[]{:S(2)}) copy-start(f32[256,256]{1,0:T(8,128)} %param.14) | copy-start | bytes 786436
Sparse Core Ops, SparseCore 0:
  10.3 335.7 all-gather.1
  473.2 36.5 all-reduce.8
  512.4 633.0 all-reduce.6
